TPU v7x, 32 devices: a whole 2x2x4 slice. The times are simulated.
32 devices in a mesh: row: 4 (over y, x), col: 8 (over z, core).
Axes of the slice: x: 2, y: 2, z: 4, core: 2. Of those that a mesh axis runs over, the one named last changes fastest.
Arguments:
- queries: bfloat16 [32, 128, 512], P('row', 'col'), may hold values from -6 to 6
- keys: bfloat16 [32, 128, 512], P('row', 'col'), may hold values from -6 to 6
- values: bfloat16 [32, 128, 512], P('row', 'col'), may hold values from -6 to 6
- grad_out: bfloat16 [32, 128, 512], P('row', 'col'), may hold values from -6 to 6
- rel_bias: float32 [8, 17, 17], replicated, may hold values from -4 to 4
- occupied: int32 [4, 8], replicated, may hold values 0 or 1
Outputs:
- grad_queries: bfloat16 [32, 128, 512], P('row', 'col')
- grad_keys: bfloat16 [32, 128, 512], P('row', 'col')
- grad_values: bfloat16 [32, 128, 512], P('row', 'col')
- grad_bias: float32 [8, 17, 17], replicated
All inputs are finite; a program needn't handle non-finite values.
Results may differ from a plain program's by a relative error of at most 0.015.
Values may be sent and summed in bfloat16 or wider, within the bound.
A program may use at most 64 MiB of HBM per device.

v0:
```python
import jax
import jax.numpy as jnp
from jax import lax
from jax.sharding import PartitionSpec as P


def from_behind(value, axis, steps):
    count = lax.axis_size(axis)
    first, last = (max(0, -steps), min(count, count - steps))
    return lax.ppermute(value, axis, [(source, source + steps) for source in range(first, last)])


def with_halo(block, sides, width):
    for axis, dim in sides:
        count = lax.axis_size(axis)
        forward = [(i, i + 1) for i in range(count - 1)]
        backward = [(target, source) for source, target in forward]
        low = lax.ppermute(
            lax.slice_in_dim(block, block.shape[dim] - width, None, axis=dim), axis, forward
        )
        high = lax.ppermute(lax.slice_in_dim(block, 0, width, axis=dim), axis, backward)
        block = jnp.concatenate([low, block, high], axis=dim)
    return block


def offset_table(first_count, second_count, direction, window_span):
    table_shape = (first_count, second_count, window_span)
    first_index = lax.broadcasted_iota(jnp.int32, table_shape, 0)
    second_index = lax.broadcasted_iota(jnp.int32, table_shape, 1)
    slot_index = lax.broadcasted_iota(jnp.int32, table_shape, 2)
    return (direction * (second_index - first_index) == slot_index).astype(jnp.float32)


def expand_part(table_rows, table_cols, bias_part):
    partial_bias = jnp.einsum(
        "cqe,de->cqd", table_cols, bias_part, preferred_element_type=jnp.float32
    ).astype(jnp.bfloat16)
    return jnp.einsum("rpd,cqd->rcpq", table_rows, partial_bias, preferred_element_type=jnp.float32)


def expand_bias(table_rows, table_cols, bias_head):
    rows_low = table_rows.astype(jnp.bfloat16)
    cols_low = table_cols.astype(jnp.bfloat16)
    bias_high = bias_head.astype(jnp.bfloat16)
    bias_rest = (bias_head - bias_high.astype(jnp.float32)).astype(jnp.bfloat16)
    full_bias = expand_part(rows_low, cols_low, bias_high) + expand_part(
        rows_low, cols_low, bias_rest
    )
    return full_bias.reshape(
        full_bias.shape[0] * full_bias.shape[1], full_bias.shape[2] * full_bias.shape[3]
    )


def bias_gradient(grad_grid, window_span):
    tile_rows, tile_cols, padded_rows, padded_cols = grad_grid.shape
    by_rows = jnp.transpose(grad_grid, (0, 2, 1, 3)).reshape(
        tile_rows * padded_rows, tile_cols, padded_cols
    )
    by_rows = jnp.pad(by_rows, ((0, tile_rows), (0, 0), (0, 0)))
    by_rows = by_rows.reshape(tile_rows, padded_rows + 1, tile_cols, padded_cols)[:, :window_span]
    row_summed = jnp.sum(by_rows, axis=0).reshape(window_span, tile_cols * padded_cols)
    row_summed = jnp.pad(row_summed, ((0, 0), (0, tile_cols)))
    skewed = row_summed.reshape(window_span, tile_cols, padded_cols + 1)[:, :, :window_span]
    return jnp.sum(skewed, axis=1)


def allowed_pairs(table_rows, table_cols, cell_filled):
    row_inside = jnp.sum(table_rows, axis=2)
    col_inside = jnp.sum(table_cols, axis=2)
    joint = (
        row_inside[:, None, :, None] * col_inside[None, :, None, :] * cell_filled[None, None, :, :]
    )
    return joint.reshape(joint.shape[0] * joint.shape[1], joint.shape[2] * joint.shape[3]) > 0.5


def pick_tiles(extent, radius):
    cell_shape = (extent + 2 * radius, 3)
    position = lax.broadcasted_iota(jnp.int32, cell_shape, 0)
    tile_index = lax.broadcasted_iota(jnp.int32, cell_shape, 1)
    tile_of_cell = (position >= radius).astype(jnp.int32) + (position >= radius + extent).astype(
        jnp.int32
    )
    return (tile_of_cell == tile_index).astype(jnp.float32)


def neighbour_cells(nearby, tile_rows, tile_cols, radius):
    pick_rows = pick_tiles(tile_rows, radius)
    pick_cols = pick_tiles(tile_cols, radius)
    inner_rows = jnp.dot(pick_rows, nearby, precision=lax.Precision.HIGHEST)
    return jnp.dot(inner_rows, pick_cols.T, precision=lax.Precision.HIGHEST)


def head_slice(matrix, head_index, head_width):
    return lax.dynamic_slice_in_dim(matrix, head_index * head_width, head_width, 1)


def fold_columns(partials, radius):
    interior = partials.shape[2] - 2 * radius
    from_after = from_behind(partials[:, :, :radius].astype(jnp.bfloat16), "col", -1).astype(
        jnp.float32
    )
    from_before = from_behind(
        partials[:, :, radius + interior :].astype(jnp.bfloat16), "col", 1
    ).astype(jnp.float32)
    middle = partials[:, :, radius : radius + interior]
    middle = middle.at[:, :, :radius].add(from_before)
    return middle.at[:, :, interior - radius :].add(from_after)


def fold_rows(partials, radius):
    interior = partials.shape[1] - 2 * radius
    from_after = from_behind(partials[:, :radius].astype(jnp.bfloat16), "row", -1).astype(
        jnp.float32
    )
    from_before = from_behind(
        partials[:, radius + interior :].astype(jnp.bfloat16), "row", 1
    ).astype(jnp.float32)
    middle = partials[:, radius : radius + interior]
    middle = middle.at[:, :radius].add(from_before)
    return middle.at[:, interior - radius :].add(from_after)


def transposed_dot(left_matrix, right_matrix):
    return lax.dot_general(
        left_matrix, right_matrix, (((0,), (0,)), ((), ())), preferred_element_type=jnp.float32
    )


def rows_dot(left_matrix, right_matrix):
    return lax.dot_general(
        left_matrix, right_matrix, (((1,), (1,)), ((), ())), preferred_element_type=jnp.float32
    )


def shards(queries, keys, values, grad_out, rel_bias, occupied):
    tile_rows, tile_cols, model_width = queries.shape
    head_count = rel_bias.shape[0]
    window_span = rel_bias.shape[1]
    radius = (window_span - 1) // 2
    head_width = model_width // head_count
    score_scale = head_width ** (-0.5)
    padded_rows = tile_rows + 2 * radius
    padded_cols = tile_cols + 2 * radius
    query_count = tile_rows * tile_cols
    padded_count = padded_rows * padded_cols
    row_index = lax.axis_index("row")
    col_index = lax.axis_index("col")
    nearby = lax.dynamic_slice(jnp.pad(occupied, 1), (row_index, col_index), (3, 3)).astype(
        jnp.float32
    )
    own_tile = nearby[1, 1]
    cell_filled = neighbour_cells(nearby, tile_rows, tile_cols, radius)
    key_value_halo = with_halo(jnp.stack((keys, values)), (("row", 1), ("col", 2)), radius)
    key_matrix = key_value_halo[0].reshape(padded_count, model_width)
    value_matrix = key_value_halo[1].reshape(padded_count, model_width)
    query_matrix = queries.reshape(query_count, model_width)
    grad_matrix = grad_out.reshape(query_count, model_width)
    forward_rows = offset_table(tile_rows, padded_rows, 1, window_span)
    forward_cols = offset_table(tile_cols, padded_cols, 1, window_span)
    forward_allowed = allowed_pairs(forward_rows, forward_cols, cell_filled)
    partial_shape = (padded_count, model_width)

    def query_pass(head_index, carried):
        grad_query, grad_key, grad_value, log_total, delta_all, grad_bias = carried
        query_head = head_slice(query_matrix, head_index, head_width)
        key_head = head_slice(key_matrix, head_index, head_width)
        value_head = head_slice(value_matrix, head_index, head_width)
        grad_head = head_slice(grad_matrix, head_index, head_width)
        bias_head = lax.dynamic_index_in_dim(rel_bias, head_index, 0, keepdims=False)
        scores = rows_dot(query_head, key_head) * score_scale + expand_bias(
            forward_rows, forward_cols, bias_head
        )
        scores = jnp.where(forward_allowed, scores, -jnp.inf)
        row_max = jnp.max(scores, axis=1, keepdims=True)
        exponent = jnp.exp(scores - row_max)
        row_total = jnp.sum(exponent, axis=1, keepdims=True)
        weights = exponent / row_total
        grad_weights = rows_dot(grad_head, value_head)
        row_delta = jnp.sum(weights * grad_weights, axis=1, keepdims=True)
        grad_scores = weights * (grad_weights - row_delta)
        weights_low = weights.astype(jnp.bfloat16)
        grad_scores_low = grad_scores.astype(jnp.bfloat16)
        query_term = (
            jnp.dot(grad_scores_low, key_head, preferred_element_type=jnp.float32) * score_scale
        )
        grad_query = lax.dynamic_update_slice_in_dim(
            grad_query, query_term, head_index * head_width, 1
        )
        bias_term = bias_gradient(
            grad_scores.reshape(tile_rows, tile_cols, padded_rows, padded_cols), window_span
        )
        grad_bias = lax.dynamic_update_index_in_dim(grad_bias, bias_term, head_index, 0)
        log_total = lax.dynamic_update_slice_in_dim(
            log_total, row_max + jnp.log(row_total), head_index, 1
        )
        delta_all = lax.dynamic_update_slice_in_dim(delta_all, row_delta, head_index, 1)
        key_term = transposed_dot(grad_scores_low, query_head) * score_scale
        value_term = transposed_dot(weights_low, grad_head)
        grad_key = lax.dynamic_update_slice_in_dim(grad_key, key_term, head_index * head_width, 1)
        grad_value = lax.dynamic_update_slice_in_dim(
            grad_value, value_term, head_index * head_width, 1
        )
        return (grad_query, grad_key, grad_value, log_total, delta_all, grad_bias)

    initial = (
        jnp.zeros((query_count, model_width), jnp.float32),
        jnp.zeros(partial_shape, jnp.float32),
        jnp.zeros(partial_shape, jnp.float32),
        jnp.zeros((query_count, head_count), jnp.float32),
        jnp.zeros((query_count, head_count), jnp.float32),
        jnp.zeros((head_count, window_span, window_span), jnp.float32),
    )

    def run_queries():
        return lax.fori_loop(0, head_count, query_pass, initial)

    def skip_queries():
        return initial

    grad_query, grad_key, grad_value, log_total, delta_all, grad_bias = lax.cond(
        own_tile > 0.5, run_queries, skip_queries
    )
    bias_summed = lax.psum(grad_bias, ("row", "col"))
    query_grads = grad_query.astype(jnp.bfloat16).reshape(tile_rows, tile_cols, model_width)
    partials = jnp.stack((grad_key, grad_value)).reshape(2, padded_rows, padded_cols, model_width)
    owned_grads = fold_rows(fold_columns(partials, radius), radius)
    return (
        query_grads,
        owned_grads[0].astype(jnp.bfloat16),
        owned_grads[1].astype(jnp.bfloat16),
        bias_summed,
    )


def solution(mesh):
    placed = (
        P("row", "col", None),
        P("row", "col", None),
        P("row", "col", None),
        P("row", "col", None),
        P(),
        P(),
    )
    return jax.shard_map(
        shards,
        mesh=mesh,
        in_specs=placed,
        out_specs=(P("row", "col", None), P("row", "col", None), P("row", "col", None), P()),
        check_vma=False,
    )
```

profile of v0, /device:TPU:0, one launch (start us, length us, event | category | flops | bytes accessed | tf_op | source)
XLA Modules:
  0.0 246.2 jit_solution(10566615659084771039)
XLA Ops:
  2.9 5.5 %collective-permute-start = (bf16[2,8,16,512]{3,2,1,0:T(8,128)(2,1)S(1)}, bf16[2,8,16,512]{3,2,1,0:T(8,128)(2,1)S(1)}, u32[]{:S(2)}, u32[]{:S(2)}) collective-permute-start(bf16[2,8,16,512]{3,2,1,0:T(8,128)(2,1)S(1)} %pad_maximum_fusion.2), channel_id=1, source_target_pairs={{0,8},{8,16},{16,24},{1,9},{9,17},{17,25},{2,10},{10,18},{18,26},{... | collective-permute-start | bytes 786440 | tf_op jit(solution)/shard_map/ppermute | solution.py:18
  9.4 4.2 %collective-permute-done.1 = bf16[2,8,16,512]{3,2,1,0:T(8,128)(2,1)S(1)} collective-permute-done((bf16[2,8,16,512]{3,2,1,0:T(8,128)(2,1)S(1)}, bf16[2,8,16,512]{3,2,1,0:T(8,128)(2,1)S(1)}, u32[]{:S(2)}, u32[]{:S(2)}) %collective-permute-start.1) | collective-permute-done | bytes 262176 | tf_op jit(solution)/shard_map/ppermute | solution.py:21
  19.2 2.8 %collective-permute-done.3 = bf16[2,24,8,512]{3,2,1,0:T(8,128)(2,1)S(1)} collective-permute-done((bf16[2,24,8,512]{3,2,1,0:T(8,128)(2,1)S(1)}, bf16[2,24,8,512]{3,2,1,0:T(8,128)(2,1)S(1)}, u32[]{:S(2)}, u32[]{:S(2)}) %collective-permute-start.3) | collective-permute-done | bytes 393248 | tf_op jit(solution)/shard_map/ppermute | solution.py:21
  22.3 149.8 %conditional.1 = (f32[8,17,17]{2,1,0:T(8,128)S(1)}, bf16[8,16,512]{2,1,0:T(8,128)(2,1)S(1)}, f32[1,24,32,512]{3,2,1,0:T(8,128)}, f32[1,24,32,512]{3,2,1,0:T(8,128)}) conditional(s32[]{:T(128)} %bitcast.7, () %tuple.69, (bf16[8,16,512]{2,1,0:T(8,128)(2,1)}, bf16[2,24,32,512]{3,2,1,0:T(8,128)(2,1)S(1)}, bf16[8,16,512]{2,1,0:T(8,128)(2,1)}, ...), branch_computations={%region_0.1_spmd, %region_1.11_spmd} | conditional | flops 72604152 | bytes 37085184 | solution.py:220
  28.0 138.3 %while.32 = (s32[]{:T(128)}, bf16[128,512]{0,1:T(8,128)(2,1)}, f32[768,512]{0,1:T(8,128)}, f32[768,512]{0,1:T(8,128)}, f32[8,17,17]{2,1,0:T(8,128)}, /*index=5*/...) while((s32[]{:T(128)}, bf16[128,512]{0,1:T(8,128)(2,1)}, ...), condition=%wide.region_10.10_spmd.clone, body=%wide.region_4.9_spmd.clone.sunk | while | flops 72592888 | bytes 17553728 | solution.py:215
  35.3 1.7 convolution_dynamic-update-slice_fusion.2
  40.4 2.0 copy.96
  57.7 2.0 copy.96
  74.9 2.0 copy.96
  87.2 1.7 convolution_dynamic-update-slice_fusion.2
  92.2 2.0 copy.96
  106.2 1.7 fusion.97
  109.5 2.0 copy.96
  126.8 2.0 copy.96
  139.0 1.7 convolution_dynamic-update-slice_fusion.2
  144.1 2.0 copy.96
  156.3 1.7 convolution_dynamic-update-slice_fusion.2
  158.0 1.7 fusion.97
  161.4 2.0 copy.96
  167.2 3.1 %copy.54 = f32[768,512]{1,0:T(8,128)} copy(f32[768,512]{0,1:T(8,128)} %get-tuple-element.464) | data formatting | bytes 3145728 | tf_op jit(solution)/shard_map/cond/branch_1_fun/while | solution.py:215
  175.5 7.9 %collective-permute-start.4 = (bf16[2,24,8,512]{3,2,1,0:T(8,128)(2,1)S(1)}, bf16[2,24,8,512]{3,2,1,0:T(8,128)(2,1)S(1)}, u32[]{:S(2)}, u32[]{:S(2)}) collective-permute-start(bf16[2,24,8,512]{3,2,1,0:T(8,128)(2,1)S(1)} %get-tuple-element.623), channel_id=1, source_target_pairs={{0,1},{1,2},{2,3},{3,4},{4,5},{5,6},{6,7},{8,9},{9,10},{10,11},{11... | collective-permute-start | bytes 1179656 | tf_op jit(solution)/shard_map/ppermute | solution.py:10
  184.9 2.0 collective-permute-done.5
  187.4 5.2 %collective-permute-start.6 = (bf16[2,8,16,512]{3,2,1,0:T(8,128)(2,1)S(1)}, bf16[2,8,16,512]{3,2,1,0:T(8,128)(2,1)S(1)}, u32[]{:S(2)}, u32[]{:S(2)}) collective-permute-start(bf16[2,8,16,512]{3,2,1,0:T(8,128)(2,1)S(1)} %get-tuple-element.624), channel_id=1, source_target_pairs={{0,8},{8,16},{16,24},{1,9},{9,17},{17,25},{2,10},{10,18},{18,26},{... | collective-permute-start | bytes 786440 | tf_op jit(solution)/shard_map/ppermute | solution.py:10
  193.9 51.5 %psum.7 = f32[8,17,17]{2,0,1:T(8,128)} all-reduce(f32[8,17,17]{2,0,1:T(8,128)S(1)} %copy.61), channel_id=1, replica_groups=mesh['row'=4,'col'=8] {'row','col'}, use_global_device_ids=true, to_apply=%region_11.12 | all-reduce | flops 2312 | bytes 18496 | tf_op jit(solution)/shard_map/psum | solution.py:223
  (262 shorter events, 135.1 us)
Async XLA Ops:
  1.6 12.0 %collective-permute-start.1 = (bf16[2,8,16,512]{3,2,1,0:T(8,128)(2,1)S(1)}, bf16[2,8,16,512]{3,2,1,0:T(8,128)(2,1)S(1)}, u32[]{:S(2)}, u32[]{:S(2)}) collective-permute-start(bf16[2,8,16,512]{3,2,1,0:T(8,128)(2,1)S(1)} %pad_maximum_fusion.2), channel_id=1, source_target_pairs={{8,0},{16,8},{24,16},{9,1},{17,9},{25,17},{10,2},{18,10},{26,18},{... | collective-permute-start | bytes 786440 | tf_op jit(solution)/shard_map/ppermute | solution.py:21
  2.9 11.1 %collective-permute-start = (bf16[2,8,16,512]{3,2,1,0:T(8,128)(2,1)S(1)}, bf16[2,8,16,512]{3,2,1,0:T(8,128)(2,1)S(1)}, u32[]{:S(2)}, u32[]{:S(2)}) collective-permute-start(bf16[2,8,16,512]{3,2,1,0:T(8,128)(2,1)S(1)} %pad_maximum_fusion.2), channel_id=1, source_target_pairs={{0,8},{8,16},{16,24},{1,9},{9,17},{17,25},{2,10},{10,18},{18,26},{... | collective-permute-start | bytes 786440 | tf_op jit(solution)/shard_map/ppermute | solution.py:18
  9.4 12.6 %copy-start.3 = (bf16[8,16,512]{2,1,0:T(8,128)(2,1)S(1)}, bf16[8,16,512]{2,1,0:T(8,128)(2,1)}, u32[]{:S(2)}) copy-start(bf16[8,16,512]{2,1,0:T(8,128)(2,1)} %param.24) | copy-start | bytes 393220
  9.4 12.6 %copy-start.4 = (bf16[8,16,512]{2,1,0:T(8,128)(2,1)S(1)}, bf16[8,16,512]{2,1,0:T(8,128)(2,1)}, u32[]{:S(2)}) copy-start(bf16[8,16,512]{2,1,0:T(8,128)(2,1)} %param.23) | copy-start | bytes 393220
  15.1 4.1 %collective-permute-start.2 = (bf16[2,24,8,512]{3,2,1,0:T(8,128)(2,1)S(1)}, bf16[2,24,8,512]{3,2,1,0:T(8,128)(2,1)S(1)}, u32[]{:S(2)}, u32[]{:S(2)}) collective-permute-start(bf16[2,24,8,512]{3,2,1,0:T(8,128)(2,1)S(1)} %get-tuple-element.626), channel_id=1, source_target_pairs={{0,1},{1,2},{2,3},{3,4},{4,5},{5,6},{6,7},{8,9},{9,10},{10,11},{11... | collective-permute-start | bytes 1179656 | tf_op jit(solution)/shard_map/ppermute | solution.py:18
  16.4 5.6 %collective-permute-start.3 = (bf16[2,24,8,512]{3,2,1,0:T(8,128)(2,1)S(1)}, bf16[2,24,8,512]{3,2,1,0:T(8,128)(2,1)S(1)}, u32[]{:S(2)}, u32[]{:S(2)}) collective-permute-start(bf16[2,24,8,512]{3,2,1,0:T(8,128)(2,1)S(1)} %get-tuple-element.627), channel_id=1, source_target_pairs={{1,0},{2,1},{3,2},{4,3},{5,4},{6,5},{7,6},{9,8},{10,9},{11,10},{12... | collective-permute-start | bytes 1179656 | tf_op jit(solution)/shard_map/ppermute | solution.py:21
  25.4 2.5 %copy-start.2 = (bf16[8,24,17]{2,1,0:T(8,128)(2,1)S(1)}, bf16[8,24,17]{2,1,0:T(8,128)(2,1)}, u32[]{:S(2)}) copy-start(bf16[8,24,17]{2,1,0:T(8,128)(2,1)} %copy.58) | copy-start | bytes 19588 | tf_op jit(solution)/shard_map/cond
  30.3 1.1 copy-start
  47.6 1.1 copy-start
  64.9 1.1 copy-start
  82.2 1.1 copy-start
  99.5 1.1 copy-start
  116.8 1.1 copy-start
  134.0 1.1 copy-start
  151.3 1.1 copy-start
  167.2 3.2 %copy-start.1 = (f32[768,512]{0,1:T(8,128)S(1)}, f32[768,512]{0,1:T(8,128)}, u32[]{:S(2)}) copy-start(f32[768,512]{0,1:T(8,128)} %get-tuple-element.465) | copy-start | bytes 4718596 | tf_op jit(solution)/shard_map/cond
  170.4 1.6 copy-start.5
  172.0 1.6 copy-start.6
  175.5 9.3 %collective-permute-start.4 = (bf16[2,24,8,512]{3,2,1,0:T(8,128)(2,1)S(1)}, bf16[2,24,8,512]{3,2,1,0:T(8,128)(2,1)S(1)}, u32[]{:S(2)}, u32[]{:S(2)}) collective-permute-start(bf16[2,24,8,512]{3,2,1,0:T(8,128)(2,1)S(1)} %get-tuple-element.623), channel_id=1, source_target_pairs={{0,1},{1,2},{2,3},{3,4},{4,5},{5,6},{6,7},{8,9},{9,10},{10,11},{11... | collective-permute-start | bytes 1179656 | tf_op jit(solution)/shard_map/ppermute | solution.py:10
  183.4 3.6 %collective-permute-start.5 = (bf16[2,24,8,512]{3,2,1,0:T(8,128)(2,1)S(1)}, bf16[2,24,8,512]{3,2,1,0:T(8,128)(2,1)S(1)}, u32[]{:S(2)}, u32[]{:S(2)}) collective-permute-start(bf16[2,24,8,512]{3,2,1,0:T(8,128)(2,1)S(1)} %get-tuple-element.622), channel_id=1, source_target_pairs={{1,0},{2,1},{3,2},{4,3},{5,4},{6,5},{7,6},{9,8},{10,9},{11,10},{12... | collective-permute-start | bytes 1179656 | tf_op jit(solution)/shard_map/ppermute | solution.py:10
  187.4 58.0 %collective-permute-start.6 = (bf16[2,8,16,512]{3,2,1,0:T(8,128)(2,1)S(1)}, bf16[2,8,16,512]{3,2,1,0:T(8,128)(2,1)S(1)}, u32[]{:S(2)}, u32[]{:S(2)}) collective-permute-start(bf16[2,8,16,512]{3,2,1,0:T(8,128)(2,1)S(1)} %get-tuple-element.624), channel_id=1, source_target_pairs={{0,8},{8,16},{16,24},{1,9},{9,17},{17,25},{2,10},{10,18},{18,26},{... | collective-permute-start | bytes 786440 | tf_op jit(solution)/shard_map/ppermute | solution.py:10
  192.6 52.8 %collective-permute-start.7 = (bf16[2,8,16,512]{3,2,1,0:T(8,128)(2,1)S(1)}, bf16[2,8,16,512]{3,2,1,0:T(8,128)(2,1)S(1)}, u32[]{:S(2)}, u32[]{:S(2)}) collective-permute-start(bf16[2,8,16,512]{3,2,1,0:T(8,128)(2,1)S(1)} %get-tuple-element.625), channel_id=1, source_target_pairs={{8,0},{16,8},{24,16},{9,1},{17,9},{25,17},{10,2},{18,10},{26,18},{... | collective-permute-start | bytes 786440 | tf_op jit(solution)/shard_map/ppermute | solution.py:10
where the time goes:
time: 249 us; the launch traced here: 246 us
  local copies, waits for them, and re-layouts  81.1 us (33%)
  matrix products  62.9 us (25%)
  blocking collectives  51.5 us (21%)
  starting transfers between devices  25.1 us (10%)
  other arithmetic  13.7 us (6%)
  waiting for transfers between devices  9.44 us (4%)
    psum x1, blocking collectives, shards(): bias_summed = lax.psum(grad_bias, ('row', 'col'))  51.5 us
    reshape x16, local copies, waits for them, and re-layouts, query_pass(): grad_scores.reshape(tile_rows, tile_cols, padded_rows, padded_cols)  28.7 us
    dot_general x16, matrix products, transposed_dot(): lax.dot_general(left_matrix, right_matrix, (((0,), (0,)), ((), ())), pref...  27.6 us
    dot_general x16, matrix products, rows_dot(): lax.dot_general(left_matrix, right_matrix, (((1,), (1,)), ((), ())), pref...  19.8 us
    ppermute x4, starting transfers between devices, from_behind(): lax.ppermute(value, axis, [(source, source + steps) for source in range(f...  15.7 us
    dot_general x8, matrix products, query_pass(): jnp.dot(grad_scores_low, key_head, preferred_element_type=jnp.float32)  7.59 us
    dot_general x16, matrix products, expand_part(): jnp.einsum('rpd,cqd->rcpq', table_rows, partial_bias, preferred_element_t...  7.48 us
    dynamic_slice x8, local copies, waits for them, and re-layouts, query_pass(): lax.dynamic_index_in_dim(rel_bias, head_index, 0, keepdims=False)  7.13 us
  transfers between devices with their start and end apart: 8, of which 4 were waited for; matrix products, arithmetic and copies ran while one was open for 1% of the time, Pallas kernels for 0%

commit v1 on v0

v1 whole, which is shorter than its diff:
```python
import functools

import jax
import jax.numpy as jnp
from jax import lax
from jax.experimental import pallas as pl
from jax.experimental.pallas import tpu as pltpu
from jax.sharding import PartitionSpec as P

MESH = pl.DeviceIdType.MESH
LANES = 128
MASKED = -1e30


def skew_rows(block, direction):
    row = lax.broadcasted_iota(jnp.int32, block.shape, 0)
    span = block.shape[1]
    bit = 1
    while bit < block.shape[0]:
        moved = pltpu.roll(block, (direction * bit) % span, 1)
        block = jnp.where((row & bit) != 0, moved, block)
        bit *= 2
    return block


def kernel(
    cfg,
    q_ref, k_ref, v_ref, g_ref, flat_ref, key_ok_ref, own_ref,
    dq_ref, dk_ref, dv_ref, db_ref,
    row_kv, col_kv, col_out, grad_col_out, grad_col_in, grad_row_out, grad_row_in,
    mid, bias_full, s_buf, gw_buf, w_buf, ds_buf, bias_acc, bias_cols, bias_rows,
    row_kv_s, row_kv_r, col_kv_s, col_kv_r, gc_s, gc_r, gr_s, gr_r, bc_s, bc_r, br_s, br_r,
):
    n_row, n_col, tr, tc, rad, heads, width = cfg
    hd = width // heads
    per = LANES // hd
    groups = width // LANES
    pr, pc = tr + 2 * rad, tc + 2 * rad
    span = pr * pc
    nq = tr * tc
    half = rad * tr
    f32, bf16 = jnp.float32, jnp.bfloat16
    r = lax.axis_index("row")
    c = lax.axis_index("col")
    row_has = (r > 0, r < n_row - 1)
    row_to = (r - 1, r + 1)
    col_has = (c > 0, c < n_col - 1)
    col_to = (c - 1, c + 1)

    row_kv[...] = jnp.zeros_like(row_kv)
    col_kv[...] = jnp.zeros_like(col_kv)
    grad_col_in[...] = jnp.zeros_like(grad_col_in)
    grad_row_in[...] = jnp.zeros_like(grad_row_in)

    barrier = pltpu.get_barrier_semaphore()
    for step in range(1, n_col):
        pl.semaphore_signal(barrier, 1, device_id=(r, lax.rem(c + step, n_col)), device_id_type=MESH)
    for step in range(1, n_row):
        pl.semaphore_signal(barrier, 1, device_id=(lax.rem(r + step, n_row), c), device_id_type=MESH)
    pl.semaphore_wait(barrier, n_col + n_row - 2)

    pending = []

    def send(cond, make):
        @pl.when(cond)
        def _():
            make().start()

        pending.append((cond, make))

    def arrived(cond, make):
        @pl.when(cond)
        def _():
            make().wait_recv()

    def lanes(g):
        return pl.ds(g * LANES, LANES)

    def row_copy(g, d, i):
        src = (k_ref, v_ref)[i]
        return lambda: pltpu.make_async_remote_copy(
            src_ref=src.at[:, lanes(g)], dst_ref=row_kv.at[1 - d, g, i],
            send_sem=row_kv_s.at[d, g, i], recv_sem=row_kv_r.at[1 - d, g, i],
            device_id=(row_to[d], c), device_id_type=MESH)

    def row_wait(g, d, i):
        arrived(row_has[d], lambda: pltpu.make_async_remote_copy(
            src_ref=row_kv.at[d, g, i], dst_ref=row_kv.at[d, g, i],
            send_sem=row_kv_s.at[d, g, i], recv_sem=row_kv_r.at[d, g, i],
            device_id=(row_to[d], c), device_id_type=MESH))

    def tile_of(g, piece, i):
        if piece == 1:
            return (k_ref, v_ref)[i][:, lanes(g)].astype(f32).reshape(tr, tc, LANES)
        return row_kv[0 if piece == 0 else 1, g, i].astype(f32).reshape(tr, tc, LANES)

    def col_copy(g, piece, d):
        return lambda: pltpu.make_async_remote_copy(
            src_ref=col_out.at[d, g, piece], dst_ref=col_kv.at[1 - d, g, piece],
            send_sem=col_kv_s.at[d, g, piece], recv_sem=col_kv_r.at[1 - d, g, piece],
            device_id=(r, col_to[d]), device_id_type=MESH)

    def col_send(g, piece):
        for i in range(2):
            tile = tile_of(g, piece, i)
            col_out[0, g, piece, i] = tile[:, :rad].reshape(half, LANES).astype(bf16)
            col_out[1, g, piece, i] = tile[:, tc - rad:].reshape(half, LANES).astype(bf16)
        for d in range(2):
            send(col_has[d], col_copy(g, piece, d))

    def col_wait(g):
        for piece in range(3):
            for d in range(2):
                arrived(col_has[d], (lambda piece, d: lambda: pltpu.make_async_remote_copy(
                    src_ref=col_kv.at[d, g, piece], dst_ref=col_kv.at[d, g, piece],
                    send_sem=col_kv_s.at[d, g, piece], recv_sem=col_kv_r.at[d, g, piece],
                    device_id=(r, col_to[d]), device_id_type=MESH))(piece, d))

    def row_stage(g):
        for d in range(2):
            for i in range(2):
                row_wait(g, d, i)
        col_send(g, 0)
        col_send(g, 2)

    def window(g, i):
        parts = []
        for piece in range(3):
            left = col_kv[0, g, piece, i].astype(f32).reshape(tr, rad, LANES)
            right = col_kv[1, g, piece, i].astype(f32).reshape(tr, rad, LANES)
            parts.append(jnp.concatenate([left, tile_of(g, piece, i), right], axis=1))
        return jnp.concatenate(parts, axis=0).reshape(span, LANES).astype(bf16)

    def stacked(matrix, scale):
        lane = lax.broadcasted_iota(jnp.int32, (nq, LANES), 1)
        wide = matrix.astype(f32) * scale
        return jnp.concatenate(
            [jnp.where(lane // hd == h, wide, 0.0) for h in range(per)], axis=0).astype(bf16)

    def expand_bias():
        lane = lax.broadcasted_iota(jnp.int32, (tc, span), 1)
        key_col = lax.rem(lane, pc)
        key_row = lane // pc
        query_col = lax.broadcasted_iota(jnp.int32, (tc, span), 0)
        off_col = key_col - query_col
        ok_col = (off_col >= 0) & (off_col <= 2 * rad) & (key_ok_ref[...] > 0.5)

        def one_head(h, _):
            base = jnp.broadcast_to(flat_ref[pl.ds(h, 1), :], (tc, span))
            base = skew_rows(base, 1)
            for qr in range(tr):
                off_row = key_row - qr
                ok = ok_col & (off_row >= 0) & (off_row <= 2 * rad)
                moved = pltpu.roll(base, (pc * qr) % span, 1) if qr else base
                bias_full[h, qr] = jnp.where(ok, moved, MASKED)
            return 0

        lax.fori_loop(0, heads, one_head, 0)

    def compute(g):
        kw = window(g, 0)
        vw = window(g, 1)
        qs = stacked(q_ref[:, lanes(g)], hd ** -0.5)
        gs = stacked(g_ref[:, lanes(g)], 1.0)
        nt = (((1,), (1,)), ((), ()))
        s_buf[...] = lax.dot_general(qs, kw, nt, preferred_element_type=f32)
        gw_buf[...] = lax.dot_general(gs, vw, nt, preferred_element_type=f32)
        bias_acc[...] = jnp.zeros_like(bias_acc)
        own = own_ref[0, 0]

        def chunk(qr, _):
            for h in range(per):
                at = pl.multiple_of(h * nq + qr * tc, tc)
                s = s_buf[pl.ds(at, tc), :] + bias_full[g * per + h, qr]
                e = jnp.exp(s - jnp.max(s, axis=1, keepdims=True))
                w = e * (own / jnp.sum(e, axis=1, keepdims=True))
                gw = gw_buf[pl.ds(at, tc), :]
                ds = w * (gw - jnp.sum(w * gw, axis=1, keepdims=True))
                w_buf[pl.ds(at, tc), :] = w.astype(bf16)
                ds_buf[pl.ds(at, tc), :] = ds.astype(bf16)
                bias_acc[h] += pltpu.roll(ds, lax.rem(span - pc * qr, span), 1)
            return 0

        lax.fori_loop(0, tr, chunk, 0)
        for h in range(per):
            total = jnp.sum(skew_rows(bias_acc[h], -1), axis=0, keepdims=True)
            bias_cols[c, pl.ds(g * per + h, 1), :] = total
        ds_low = ds_buf[...]
        tn = (((0,), (0,)), ((), ()))
        dq = jnp.dot(ds_low, kw, preferred_element_type=f32) * (hd ** -0.5)
        lane = lax.broadcasted_iota(jnp.int32, (nq, LANES), 1)
        merged = dq[:nq]
        for h in range(1, per):
            merged = jnp.where(lane // hd == h, dq[h * nq:(h + 1) * nq], merged)
        dq_ref[:, lanes(g)] = merged.astype(bf16)
        for i, (left, right) in enumerate(((ds_low, qs), (w_buf[...], gs))):
            full = lax.dot_general(left, right, tn, preferred_element_type=f32)
            full = full.reshape(pr, pc, LANES)
            grad_col_out[0, g, i] = full[:, :rad].reshape(pr * rad, LANES).astype(bf16)
            grad_col_out[1, g, i] = full[:, rad + tc:].reshape(pr * rad, LANES).astype(bf16)
            mid[g, i] = full[:, rad:rad + tc]
        for d in range(2):
            send(col_has[d], (lambda d: lambda: pltpu.make_async_remote_copy(
                src_ref=grad_col_out.at[d, g], dst_ref=grad_col_in.at[1 - d, g],
                send_sem=gc_s.at[d, g], recv_sem=gc_r.at[1 - d, g],
                device_id=(r, col_to[d]), device_id_type=MESH))(d))

    def col_return(g):
        for d in range(2):
            arrived(col_has[d], (lambda d: lambda: pltpu.make_async_remote_copy(
                src_ref=grad_col_in.at[d, g], dst_ref=grad_col_in.at[d, g],
                send_sem=gc_s.at[d, g], recv_sem=gc_r.at[d, g],
                device_id=(r, col_to[d]), device_id_type=MESH))(d))
        for i in range(2):
            sides = [grad_col_in[d, g, i].astype(f32).reshape(pr, rad, LANES) for d in range(2)]
            if tc == 2 * rad:
                total = mid[g, i] + jnp.concatenate(sides, axis=1)
            else:
                gap = jnp.zeros((pr, tc - rad, LANES), f32)
                total = (mid[g, i] + jnp.concatenate([sides[0], gap], axis=1)
                         + jnp.concatenate([gap, sides[1]], axis=1))
            grad_row_out[0, g, i] = total[:rad].reshape(nq, LANES).astype(bf16)
            grad_row_out[1, g, i] = total[rad + tr:].reshape(nq, LANES).astype(bf16)
            mid[g, i] = total
        for d in range(2):
            send(row_has[d], (lambda d: lambda: pltpu.make_async_remote_copy(
                src_ref=grad_row_out.at[d, g], dst_ref=grad_row_in.at[1 - d, g],
                send_sem=gr_s.at[d, g], recv_sem=gr_r.at[1 - d, g],
                device_id=(row_to[d], c), device_id_type=MESH))(d))

    def finish(g):
        for d in range(2):
            arrived(row_has[d], (lambda d: lambda: pltpu.make_async_remote_copy(
                src_ref=grad_row_in.at[d, g], dst_ref=grad_row_in.at[d, g],
                send_sem=gr_s.at[d, g], recv_sem=gr_r.at[d, g],
                device_id=(row_to[d], c), device_id_type=MESH))(d))
        for i, out in enumerate((dk_ref, dv_ref)):
            total = mid[g, i, pl.ds(rad, tr)].reshape(nq, LANES)
            total = total + grad_row_in[0, g, i].astype(f32) + grad_row_in[1, g, i].astype(f32)
            out[:, lanes(g)] = total.astype(bf16)

    for g in range(groups):
        for d in range(2):
            for i in range(2):
                send(row_has[d], row_copy(g, d, i))
    for g in range(groups):
        col_send(g, 1)
    expand_bias()
    row_stage(0)
    for g in range(groups):
        if g + 1 < groups:
            row_stage(g + 1)
        col_wait(g)
        compute(g)
        if g >= 1:
            col_return(g - 1)
        if g >= 2:
            finish(g - 2)

    def bias_copies(buf, mine, count, send_sem, recv_sem, device):
        return [pltpu.make_async_remote_copy(
            src_ref=buf.at[mine], dst_ref=buf.at[mine],
            send_sem=send_sem.at[step], recv_sem=recv_sem.at[step],
            device_id=device(lax.rem(mine + step, count)), device_id_type=MESH)
            for step in range(1, count)]

    def bias_waits(buf, mine, count, send_sem, recv_sem, device):
        for step in range(1, count):
            source = lax.rem(mine + count - step, count)
            pltpu.make_async_remote_copy(
                src_ref=buf.at[source], dst_ref=buf.at[source],
                send_sem=send_sem.at[step], recv_sem=recv_sem.at[step],
                device_id=device(source), device_id_type=MESH).wait_recv()

    by_col = (bias_cols, c, n_col, bc_s, bc_r, lambda at: (r, at))
    by_row = (bias_rows, r, n_row, br_s, br_r, lambda at: (at, c))
    col_copies = bias_copies(*by_col)
    for copy in col_copies:
        copy.start()
    col_return(groups - 1)
    if groups >= 2:
        finish(groups - 2)
    bias_waits(*by_col)
    total = bias_cols[0]
    for at in range(1, n_col):
        total = total + bias_cols[at]
    bias_rows[r] = total
    row_copies = bias_copies(*by_row)
    for copy in row_copies:
        copy.start()
    finish(groups - 1)
    bias_waits(*by_row)
    total = bias_rows[0]
    for at in range(1, n_row):
        total = total + bias_rows[at]
    db_ref[...] = total
    for copy in col_copies + row_copies:
        copy.wait_send()
    for cond, make in pending:
        @pl.when(cond)
        def _():
            make().wait_send()


def shards(n_row, n_col, queries, keys, values, grad_out, rel_bias, occupied):
    tr, tc, width = queries.shape
    heads, win, _ = rel_bias.shape
    rad = (win - 1) // 2
    pr, pc = tr + 2 * rad, tc + 2 * rad
    span = pr * pc
    nq = tr * tc
    groups = width // LANES
    per = heads // groups
    half = rad * tr
    r = lax.axis_index("row")
    c = lax.axis_index("col")
    nearby = lax.dynamic_slice(jnp.pad(occupied, 1), (r, c), (3, 3)).astype(jnp.float32)
    row_tile = [0] * rad + [1] * tr + [2] * rad
    col_tile = [0] * rad + [1] * tc + [2] * rad
    rows = jnp.concatenate([jnp.broadcast_to(nearby[i:i + 1], (n, 3)) for i, n in enumerate((rad, tr, rad))], axis=0)
    cells = jnp.concatenate(
        [jnp.broadcast_to(rows[:, i:i + 1], (pr, n)) for i, n in enumerate((rad, tc, rad))], axis=1)
    key_ok = cells.reshape(1, span)
    own = nearby[1:2, 1:2]
    flat = jnp.pad(rel_bias, ((0, 0), (0, pr - win), (0, pc - win))).reshape(heads, span)
    f32, bf16 = jnp.float32, jnp.bfloat16
    vmem = pl.BlockSpec(memory_space=pltpu.VMEM)
    dma = pltpu.SemaphoreType.DMA
    token = jax.ShapeDtypeStruct((nq, width), bf16)
    cfg = (n_row, n_col, tr, tc, rad, heads, width)
    dq, dk, dv, db = pl.pallas_call(
        functools.partial(kernel, cfg),
        out_shape=(token, token, token, jax.ShapeDtypeStruct((heads, span), f32)),
        in_specs=[vmem] * 6 + [pl.BlockSpec(memory_space=pltpu.SMEM)],
        out_specs=(vmem,) * 4,
        scratch_shapes=[
            pltpu.VMEM((2, groups, 2, nq, LANES), bf16),
            pltpu.VMEM((2, groups, 3, 2, half, LANES), bf16),
            pltpu.VMEM((2, groups, 3, 2, half, LANES), bf16),
            pltpu.VMEM((2, groups, 2, pr * rad, LANES), bf16),
            pltpu.VMEM((2, groups, 2, pr * rad, LANES), bf16),
            pltpu.VMEM((2, groups, 2, nq, LANES), bf16),
            pltpu.VMEM((2, groups, 2, nq, LANES), bf16),
            pltpu.VMEM((groups, 2, pr, tc, LANES), f32),
            pltpu.VMEM((heads, tr, tc, span), f32),
            pltpu.VMEM((per * nq, span), f32),
            pltpu.VMEM((per * nq, span), f32),
            pltpu.VMEM((per * nq, span), bf16),
            pltpu.VMEM((per * nq, span), bf16),
            pltpu.VMEM((per, tc, span), f32),
            pltpu.VMEM((n_col, heads, span), f32),
            pltpu.VMEM((n_row, heads, span), f32),
            dma((2, groups, 2)), dma((2, groups, 2)),
            dma((2, groups, 3)), dma((2, groups, 3)),
            dma((2, groups)), dma((2, groups)),
            dma((2, groups)), dma((2, groups)),
            dma((n_col,)), dma((n_col,)),
            dma((n_row,)), dma((n_row,)),
        ],
        compiler_params=pltpu.CompilerParams(
            collective_id=0, has_side_effects=True, vmem_limit_bytes=48 * 1024 * 1024),
    )(
        queries.reshape(nq, width), keys.reshape(nq, width), values.reshape(nq, width),
        grad_out.reshape(nq, width), flat, key_ok, own,
    )
    grad_bias = db.reshape(heads, pr, pc)[:, :win, :win]
    shape = (tr, tc, width)
    return dq.reshape(shape), dk.reshape(shape), dv.reshape(shape), grad_bias


def solution(mesh):
    tokens = P("row", "col", None)
    return jax.shard_map(
        functools.partial(shards, mesh.shape["row"], mesh.shape["col"]),
        mesh=mesh,
        in_specs=(tokens,) * 4 + (P(), P()),
        out_specs=(tokens,) * 3 + (P(),),
        check_vma=False,
    )
```

time: 249 us -> 48.4 us (0.19); the launches traced: 246 us -> 48.2 us
  local copies, waits for them, and re-layouts: 81.1 us -> 5.39 us
  matrix products: 62.9 us -> 0 us
  blocking collectives: 51.5 us -> 0 us
  Pallas kernels: 0 us -> 41.9 us
  starting transfers between devices: 25.1 us -> 0 us
  other arithmetic: 13.7 us -> 0.24 us
  waiting for transfers between devices: 9.44 us -> 0 us
    dot_general x58 -> x0, matrix products: 62.9 us -> none  [the longest x16 27.6 us: transposed_dot(): lax.dot_general(left_matrix, right_matrix, (((0,), (0,)), ((), ())), pref...]
    psum x1 -> x0, blocking collectives: 51.5 us -> none  [shards(): bias_summed = lax.psum(grad_bias, ('row', 'col'))]
    reshape x56 -> x3, local copies, waits for them, and re-layouts: 44.1 us -> 0.25 us  [the longest x1 0.09 us: shards(): jnp.pad(rel_bias, ((0, 0), (0, pr - win), (0, pc - win)))]
    pallas_call x0 -> x1, Pallas kernels: none -> 41.9 us  [shards(): pl.pallas_call(functools.partial(kernel, cfg), out_shape=(token, token, t...]
    ppermute x8 -> x0, starting transfers between devices: 25.1 us -> none  [the longest x4 15.7 us: from_behind(): lax.ppermute(value, axis, [(source, source + steps) for source in range(f...]
    while x19 -> x0, local copies, waits for them, and re-layouts: 10.1 us -> none  [the longest x3 5.77 us: run_queries(): return lax.fori_loop(0, head_count, query_pass, initial)]
    ppermute x8 -> x0, waiting for transfers between devices: 9.44 us -> none  [the longest x2 7.05 us: with_halo(): lax.ppermute(lax.slice_in_dim(block, 0, width, axis=dim), axis, backward)]
    dynamic_slice x8 -> x0, local copies, waits for them, and re-layouts: 7.13 us -> none  [query_pass(): lax.dynamic_index_in_dim(rel_bias, head_index, 0, keepdims=False)]
  transfers between devices with their start and end apart: 8 -> 0, of which waited for: 4 -> 0; matrix products, arithmetic and copies ran while one was open for 1% -> 0% of each run, Pallas kernels for 0% -> 0%
where the time goes in v1:
time: 48.4 us; the launch traced here: 48.2 us
  Pallas kernels  41.9 us (87%)
  local copies, waits for them, and re-layouts  5.39 us (11%)
  between operations  0.71 us (1%)
    pallas_call x1, Pallas kernels, shards(): pl.pallas_call(functools.partial(kernel, cfg), out_shape=(token, token, t...  41.9 us
    unnamed x15, local copies, waits for them, and re-layouts  4.1 us

profile of v1, /device:TPU:0, one launch (start us, length us, event | category | flops | bytes accessed | tf_op | source)
XLA Modules:
  0.0 48.2 jit_solution(11476043565143458253)
XLA Ops:
  0.6 0.9 %copy.13 = f32[8,17,17]{2,1,0:T(8,128)S(1)} copy(f32[8,17,17]{2,0,1:T(8,128)} %param.10) | data formatting | bytes 18496
  1.6 0.0 copy-start.4
  1.6 0.0 copy-start.2
  1.6 0.0 copy-start
  1.6 0.0 copy-start.1
  1.6 0.1 reshape.42.flat_ref
  1.7 0.5 %copy-done.4 = s32[4,8]{1,0:T(4,128)S(1)} copy-done((s32[4,8]{1,0:T(4,128)S(1)}, s32[4,8]{1,0:T(4,128)}, u32[]{:S(2)}) %copy-start.4) | copy-done | bytes 152
  2.3 0.1 fusion
  2.4 0.1 broadcast_in_dim.47
  2.4 0.1 broadcast_in_dim.45
  2.5 0.1 broadcast_in_dim.43
  2.6 0.1 pad_maximum_fusion.1
  2.7 0.1 broadcast_in_dim.53
  2.7 0.1 broadcast_in_dim.51
  2.8 0.1 broadcast_in_dim.49
  2.9 0.1 pad_maximum_fusion
  2.9 0.1 reshape.43.key_ok_ref
  3.0 0.6 %slice.30.own_ref = f32[1,1]{1,0:T(1,128)} slice(f32[3,3]{1,0:T(4,128)S(1)} %fusion), slice={[1:2], [1:2]} | slice | bytes 8 | tf_op jit(solution)/shard_map/slice | solution.py:324
  3.6 41.9 %shard_map.93 = (bf16[128,512]{1,0:T(8,128)(2,1)S(1)}, bf16[128,512]{1,0:T(8,128)(2,1)S(1)}, bf16[128,512]{1,0:T(8,128)(2,1)S(1)}, f32[8,768]{1,0:T(8,128)S(1)}) custom-call(bf16[128,512]{1,0:T(8,128)(2,1)S(1)} %bitcast.20, bf16[128,512]{1,0:T(8,128)(2,1)S(1)} %bitcast.21, bf16[128,512]{1,0:T(8,128)(2,1)S(1)} %bitcast.22, bf16[128,512]{1,0:T(8,128)(2,1)S(1)} %bitcast.23, ...), custom_call_target="tpu_custom_call" | custom-call | tf_op jit(solution)/shard_map/pallas_call | solution.py:331
  45.5 0.1 reshape.47
  45.6 0.6 %copy.12 = f32[8,17,17]{2,0,1:T(8,128)} copy(f32[8,17,17]{2,1,0:T(8,128)S(1)} %bitcast.27) | data formatting | bytes 18496
  46.3 0.7 %copy.17 = bf16[8,16,512]{2,1,0:T(8,128)(2,1)} copy(bf16[8,16,512]{2,1,0:T(8,128)(2,1)S(1)} %bitcast.26) | data formatting | bytes 262144
  46.9 0.7 %copy.18 = bf16[8,16,512]{2,1,0:T(8,128)(2,1)} copy(bf16[8,16,512]{2,1,0:T(8,128)(2,1)S(1)} %bitcast.25) | data formatting | bytes 262144
  47.6 0.7 %copy.19 = bf16[8,16,512]{2,1,0:T(8,128)(2,1)} copy(bf16[8,16,512]{2,1,0:T(8,128)(2,1)S(1)} %bitcast.24) | data formatting | bytes 262144
  (8 shorter events, 0.0 us)
Async XLA Ops:
  0.6 3.0 %copy-start.3 = (bf16[8,16,512]{2,1,0:T(8,128)(2,1)S(1)}, bf16[8,16,512]{2,1,0:T(8,128)(2,1)}, u32[]{:S(2)}) copy-start(bf16[8,16,512]{2,1,0:T(8,128)(2,1)} %param.9) | copy-start | bytes 393220
  1.6 0.7 %copy-start.4 = (s32[4,8]{1,0:T(4,128)S(1)}, s32[4,8]{1,0:T(4,128)}, u32[]{:S(2)}) copy-start(s32[4,8]{1,0:T(4,128)} %param.11) | copy-start | bytes 388
  1.6 2.0 %copy-start.2 = (bf16[8,16,512]{2,1,0:T(8,128)(2,1)S(1)}, bf16[8,16,512]{2,1,0:T(8,128)(2,1)}, u32[]{:S(2)}) copy-start(bf16[8,16,512]{2,1,0:T(8,128)(2,1)} %param.8) | copy-start | bytes 393220
  1.6 2.0 %copy-start = (bf16[8,16,512]{2,1,0:T(8,128)(2,1)S(1)}, bf16[8,16,512]{2,1,0:T(8,128)(2,1)}, u32[]{:S(2)}) copy-start(bf16[8,16,512]{2,1,0:T(8,128)(2,1)} %param.6) | copy-start | bytes 393220
  1.6 2.0 %copy-start.1 = (bf16[8,16,512]{2,1,0:T(8,128)(2,1)S(1)}, bf16[8,16,512]{2,1,0:T(8,128)(2,1)}, u32[]{:S(2)}) copy-start(bf16[8,16,512]{2,1,0:T(8,128)(2,1)} %param.7) | copy-start | bytes 393220

commit v2 on v1

--- a/solution.py
+++ b/solution.py
@@ -25,13 +25,15 @@
 
 def kernel(
     cfg,
-    q_ref, k_ref, v_ref, g_ref, flat_ref, key_ok_ref, own_ref,
-    dq_ref, dk_ref, dv_ref, db_ref,
+    q_hbm, k_hbm, v_hbm, g_hbm, bias_hbm, occ_hbm,
+    dq_hbm, dk_hbm, dv_hbm, db_hbm,
+    q_ref, k_ref, v_ref, g_ref, bias_ref, occ_ref, dq_ref, dk_ref, dv_ref, db_ref, in_s, out_s,
     row_kv, col_kv, col_out, grad_col_out, grad_col_in, grad_row_out, grad_row_in,
-    mid, bias_full, s_buf, gw_buf, w_buf, ds_buf, bias_acc, bias_cols, bias_rows,
+    mid, flat_ref, bias_full, s_buf, gw_buf, w_buf, ds_buf, bias_acc, bias_cols, bias_rows,
     row_kv_s, row_kv_r, col_kv_s, col_kv_r, gc_s, gc_r, gr_s, gr_r, bc_s, bc_r, br_s, br_r,
 ):
     n_row, n_col, tr, tc, rad, heads, width = cfg
+    win = 2 * rad + 1
     hd = width // heads
     per = LANES // hd
     groups = width // LANES
@@ -47,10 +49,10 @@
     col_has = (c > 0, c < n_col - 1)
     col_to = (c - 1, c + 1)
 
-    row_kv[...] = jnp.zeros_like(row_kv)
-    col_kv[...] = jnp.zeros_like(col_kv)
-    grad_col_in[...] = jnp.zeros_like(grad_col_in)
-    grad_row_in[...] = jnp.zeros_like(grad_row_in)
+    moves = ((k_hbm, k_ref), (v_hbm, v_ref), (occ_hbm, occ_ref), (bias_hbm, bias_ref), (q_hbm, q_ref), (g_hbm, g_ref))
+    loads = [pltpu.make_async_copy(a, b, in_s.at[i]) for i, (a, b) in enumerate(moves)]
+    for load in loads:
+        load.start()
 
     barrier = pltpu.get_barrier_semaphore()
     for step in range(1, n_col):
@@ -59,7 +61,10 @@
         pl.semaphore_signal(barrier, 1, device_id=(lax.rem(r + step, n_row), c), device_id_type=MESH)
     pl.semaphore_wait(barrier, n_col + n_row - 2)
 
+    for load in loads[:2]:
+        load.wait()
     pending = []
+    stores = []
 
     def send(cond, make):
         @pl.when(cond)
@@ -75,6 +80,18 @@
 
     def lanes(g):
         return pl.ds(g * LANES, LANES)
+
+    def clear_missing():
+        for d in range(2):
+            @pl.when(jnp.logical_not(row_has[d]))
+            def _():
+                row_kv[d] = jnp.zeros_like(row_kv[d])
+                grad_row_in[d] = jnp.zeros_like(grad_row_in[d])
+
+            @pl.when(jnp.logical_not(col_has[d]))
+            def _():
+                col_kv[d] = jnp.zeros_like(col_kv[d])
+                grad_col_in[d] = jnp.zeros_like(grad_col_in[d])
 
     def row_copy(g, d, i):
         src = (k_ref, v_ref)[i]
@@ -137,13 +154,32 @@
         return jnp.concatenate(
             [jnp.where(lane // hd == h, wide, 0.0) for h in range(per)], axis=0).astype(bf16)
 
+    def occupied_at(i, j):
+        at_row, at_col = r + i - 1, c + j - 1
+        inside = (at_row >= 0) & (at_row < n_row) & (at_col >= 0) & (at_col < n_col)
+        value = occ_ref[jnp.clip(at_row, 0, n_row - 1), jnp.clip(at_col, 0, n_col - 1)]
+        return jnp.where(inside, value, 0)
+
     def expand_bias():
+        fill = jnp.zeros((heads, pc - win), f32)
+        parts = []
+        for a in range(win):
+            parts += [bias_ref[a], fill]
+        flat_ref[...] = jnp.concatenate(parts + [jnp.zeros((heads, span - win * pc), f32)], axis=1)
         lane = lax.broadcasted_iota(jnp.int32, (tc, span), 1)
         key_col = lax.rem(lane, pc)
         key_row = lane // pc
         query_col = lax.broadcasted_iota(jnp.int32, (tc, span), 0)
         off_col = key_col - query_col
-        ok_col = (off_col >= 0) & (off_col <= 2 * rad) & (key_ok_ref[...] > 0.5)
+        ok_col = (off_col >= 0) & (off_col <= 2 * rad)
+        in_row = (key_row >= rad).astype(jnp.int32) + (key_row >= rad + tr).astype(jnp.int32)
+        in_col = (key_col >= rad).astype(jnp.int32) + (key_col >= rad + tc).astype(jnp.int32)
+        tile = 3 * in_row + in_col
+        key_ok = jnp.zeros((tc, span), jnp.int32)
+        for i in range(3):
+            for j in range(3):
+                key_ok = jnp.where(tile == 3 * i + j, occupied_at(i, j), key_ok)
+        ok_col = ok_col & (key_ok > 0)
 
         def one_head(h, _):
             base = jnp.broadcast_to(flat_ref[pl.ds(h, 1), :], (tc, span))
@@ -166,11 +202,11 @@
         s_buf[...] = lax.dot_general(qs, kw, nt, preferred_element_type=f32)
         gw_buf[...] = lax.dot_general(gs, vw, nt, preferred_element_type=f32)
         bias_acc[...] = jnp.zeros_like(bias_acc)
-        own = own_ref[0, 0]
-
-        def chunk(qr, _):
+        own = occ_ref[r, c].astype(f32)
+
+        for qr in range(tr):
             for h in range(per):
-                at = pl.multiple_of(h * nq + qr * tc, tc)
+                at = h * nq + qr * tc
                 s = s_buf[pl.ds(at, tc), :] + bias_full[g * per + h, qr]
                 e = jnp.exp(s - jnp.max(s, axis=1, keepdims=True))
                 w = e * (own / jnp.sum(e, axis=1, keepdims=True))
@@ -178,10 +214,8 @@
                 ds = w * (gw - jnp.sum(w * gw, axis=1, keepdims=True))
                 w_buf[pl.ds(at, tc), :] = w.astype(bf16)
                 ds_buf[pl.ds(at, tc), :] = ds.astype(bf16)
-                bias_acc[h] += pltpu.roll(ds, lax.rem(span - pc * qr, span), 1)
-            return 0
-
-        lax.fori_loop(0, tr, chunk, 0)
+                bias_acc[h] += pltpu.roll(ds, (span - pc * qr) % span, 1) if qr else ds
+
         for h in range(per):
             total = jnp.sum(skew_rows(bias_acc[h], -1), axis=0, keepdims=True)
             bias_cols[c, pl.ds(g * per + h, 1), :] = total
@@ -228,6 +262,11 @@
                 send_sem=gr_s.at[d, g], recv_sem=gr_r.at[1 - d, g],
                 device_id=(row_to[d], c), device_id_type=MESH))(d))
 
+    def store(src, dst):
+        copy = pltpu.make_async_copy(src, dst, out_s.at[len(stores)])
+        copy.start()
+        stores.append(copy)
+
     def finish(g):
         for d in range(2):
             arrived(row_has[d], (lambda d: lambda: pltpu.make_async_remote_copy(
@@ -238,6 +277,7 @@
             total = mid[g, i, pl.ds(rad, tr)].reshape(nq, LANES)
             total = total + grad_row_in[0, g, i].astype(f32) + grad_row_in[1, g, i].astype(f32)
             out[:, lanes(g)] = total.astype(bf16)
+            store(out.at[:, lanes(g)], (dk_hbm, dv_hbm)[i].at[:, lanes(g)])
 
     for g in range(groups):
         for d in range(2):
@@ -245,6 +285,9 @@
                 send(row_has[d], row_copy(g, d, i))
     for g in range(groups):
         col_send(g, 1)
+    clear_missing()
+    for load in loads[2:]:
+        load.wait()
     expand_bias()
     row_stage(0)
     for g in range(groups):
@@ -256,6 +299,8 @@
             col_return(g - 1)
         if g >= 2:
             finish(g - 2)
+
+    store(dq_ref, dq_hbm)
 
     def bias_copies(buf, mine, count, send_sem, recv_sem, device):
         return [pltpu.make_async_remote_copy(
@@ -293,13 +338,32 @@
     total = bias_rows[0]
     for at in range(1, n_row):
         total = total + bias_rows[at]
-    db_ref[...] = total
+    for a in range(win):
+        db_ref[a] = total[:, a * pc:a * pc + win]
+    store(db_ref, db_hbm)
     for copy in col_copies + row_copies:
         copy.wait_send()
+    for copy in stores:
+        copy.wait()
     for cond, make in pending:
         @pl.when(cond)
         def _():
             make().wait_send()
+
+
+def writer(*refs):
+    count = (len(refs) - 2) // 3
+    ins, outs, held = refs[:count], refs[count:2 * count], refs[2 * count:3 * count]
+    in_sems, out_sems = refs[3 * count:]
+    reads = [pltpu.make_async_copy(a, b, in_sems.at[i]) for i, (a, b) in enumerate(zip(ins, held))]
+    writes = [pltpu.make_async_copy(a, b, out_sems.at[i]) for i, (a, b) in enumerate(zip(held, outs))]
+    for read in reads:
+        read.start()
+    for read, write in zip(reads, writes):
+        read.wait()
+        write.start()
+    for write in writes:
+        write.wait()
 
 
 def shards(n_row, n_col, queries, keys, values, grad_out, rel_bias, occupied):
@@ -312,28 +376,23 @@
     groups = width // LANES
     per = heads // groups
     half = rad * tr
-    r = lax.axis_index("row")
-    c = lax.axis_index("col")
-    nearby = lax.dynamic_slice(jnp.pad(occupied, 1), (r, c), (3, 3)).astype(jnp.float32)
-    row_tile = [0] * rad + [1] * tr + [2] * rad
-    col_tile = [0] * rad + [1] * tc + [2] * rad
-    rows = jnp.concatenate([jnp.broadcast_to(nearby[i:i + 1], (n, 3)) for i, n in enumerate((rad, tr, rad))], axis=0)
-    cells = jnp.concatenate(
-        [jnp.broadcast_to(rows[:, i:i + 1], (pr, n)) for i, n in enumerate((rad, tc, rad))], axis=1)
-    key_ok = cells.reshape(1, span)
-    own = nearby[1:2, 1:2]
-    flat = jnp.pad(rel_bias, ((0, 0), (0, pr - win), (0, pc - win))).reshape(heads, span)
     f32, bf16 = jnp.float32, jnp.bfloat16
-    vmem = pl.BlockSpec(memory_space=pltpu.VMEM)
+    hbm = pl.BlockSpec(memory_space=pltpu.HBM)
     dma = pltpu.SemaphoreType.DMA
     token = jax.ShapeDtypeStruct((nq, width), bf16)
+    results = (token, token, token, jax.ShapeDtypeStruct((win, heads, win), f32))
+    held = [pltpu.VMEM(result.shape, result.dtype) for result in results]
     cfg = (n_row, n_col, tr, tc, rad, heads, width)
     dq, dk, dv, db = pl.pallas_call(
         functools.partial(kernel, cfg),
-        out_shape=(token, token, token, jax.ShapeDtypeStruct((heads, span), f32)),
-        in_specs=[vmem] * 6 + [pl.BlockSpec(memory_space=pltpu.SMEM)],
-        out_specs=(vmem,) * 4,
-        scratch_shapes=[
+        out_shape=results,
+        in_specs=[hbm] * 6,
+        out_specs=(hbm,) * 4,
+        scratch_shapes=[pltpu.VMEM((nq, width), bf16)] * 4 + [
+            pltpu.VMEM((win, heads, win), f32),
+            pltpu.SMEM(occupied.shape, jnp.int32),
+        ] + held + [
+            dma((6,)), dma((2 * groups + 2,)),
             pltpu.VMEM((2, groups, 2, nq, LANES), bf16),
             pltpu.VMEM((2, groups, 3, 2, half, LANES), bf16),
             pltpu.VMEM((2, groups, 3, 2, half, LANES), bf16),
@@ -342,6 +401,7 @@
             pltpu.VMEM((2, groups, 2, nq, LANES), bf16),
             pltpu.VMEM((2, groups, 2, nq, LANES), bf16),
             pltpu.VMEM((groups, 2, pr, tc, LANES), f32),
+            pltpu.VMEM((heads, span), f32),
             pltpu.VMEM((heads, tr, tc, span), f32),
             pltpu.VMEM((per * nq, span), f32),
             pltpu.VMEM((per * nq, span), f32),
@@ -358,14 +418,20 @@
             dma((n_row,)), dma((n_row,)),
         ],
         compiler_params=pltpu.CompilerParams(
-            collective_id=0, has_side_effects=True, vmem_limit_bytes=48 * 1024 * 1024),
+            collective_id=0, has_side_effects=True),
     )(
         queries.reshape(nq, width), keys.reshape(nq, width), values.reshape(nq, width),
-        grad_out.reshape(nq, width), flat, key_ok, own,
+        grad_out.reshape(nq, width), jnp.transpose(rel_bias, (1, 0, 2)), occupied,
     )
-    grad_bias = db.reshape(heads, pr, pc)[:, :win, :win]
+    dq, dk, dv, db = pl.pallas_call(
+        writer,
+        out_shape=results,
+        in_specs=[hbm] * 4,
+        out_specs=(hbm,) * 4,
+        scratch_shapes=held + [dma((4,)), dma((4,))],
+    )(dq, dk, dv, db)
     shape = (tr, tc, width)
-    return dq.reshape(shape), dk.reshape(shape), dv.reshape(shape), grad_bias
+    return dq.reshape(shape), dk.reshape(shape), dv.reshape(shape), jnp.transpose(db, (1, 0, 2))
 
 
 def solution(mesh):

time: 48.4 us -> 38.4 us (0.79)
  local copies, waits for them, and re-layouts: 5.39 us -> 0 us
  Pallas kernels: 41.9 us -> 37.6 us
    pallas_call x1 -> x2, Pallas kernels: 41.9 us -> 37.6 us  [the longest x1 35.9 us: shards(): pl.pallas_call(functools.partial(kernel, cfg), out_shape=results, in_spec...]
    unnamed x15 -> x0, local copies, waits for them, and re-layouts: 4.1 us -> none
    slice x1 -> x0, local copies, waits for them, and re-layouts: 0.59 us -> none  [shards(): own = nearby[1:2, 1:2]]
where the time goes in v2:
time: 38.4 us; the launch traced here: 38.3 us
  Pallas kernels  37.6 us (98%)
  between operations  0.64 us (2%)
    pallas_call x1, Pallas kernels, shards(): pl.pallas_call(functools.partial(kernel, cfg), out_shape=results, in_spec...  35.9 us
    pallas_call x1, Pallas kernels, shards(): pl.pallas_call(writer, out_shape=results, in_specs=[hbm] * 4, out_specs=(...  1.78 us

profile of v2, /device:TPU:0, one launch (start us, length us, event | category | flops | bytes accessed | tf_op | source)
XLA Modules:
  0.0 38.3 jit_solution(2873752616211271590)
XLA Ops:
  0.6 35.9 %shard_map.93 = (bf16[128,512]{1,0:T(8,128)(2,1)}, bf16[128,512]{1,0:T(8,128)(2,1)}, bf16[128,512]{1,0:T(8,128)(2,1)}, f32[17,8,17]{2,1,0:T(8,128)}) custom-call(bf16[128,512]{1,0:T(8,128)(2,1)} %bitcast.9, bf16[128,512]{1,0:T(8,128)(2,1)} %bitcast.10, bf16[128,512]{1,0:T(8,128)(2,1)} %bitcast.11, bf16[128,512]{1,0:T(8,128)(2,1)} %bitcast.12, ...), custom_call_target="tpu_custom_call" | custom-call | tf_op jit(solution)/shard_map/pallas_call | solution.py:386
  36.5 1.8 %shard_map.94 = (bf16[128,512]{1,0:T(8,128)(2,1)}, bf16[128,512]{1,0:T(8,128)(2,1)}, bf16[128,512]{1,0:T(8,128)(2,1)}, f32[17,8,17]{2,1,0:T(8,128)}) custom-call(bf16[128,512]{1,0:T(8,128)(2,1)} %get-tuple-element.12.refs_0_, bf16[128,512]{1,0:T(8,128)(2,1)} %get-tuple-element.13.refs_1_, bf16[128,512]{1,0:T(8,128)(2,1)} %get-tuple-element.14.refs_2_, ...), custom_call_target="tpu_custom_call" | custom-call | tf_op jit(solution)/shard_map/pallas_call | solution.py:426

commit v3 on v2

--- a/solution.py
+++ b/solution.py
@@ -218,7 +218,7 @@
 
         for h in range(per):
             total = jnp.sum(skew_rows(bias_acc[h], -1), axis=0, keepdims=True)
-            bias_cols[c, pl.ds(g * per + h, 1), :] = total
+            bias_cols[c, g, pl.ds(h, 1), :] = total
         ds_low = ds_buf[...]
         tn = (((0,), (0,)), ((), ()))
         dq = jnp.dot(ds_low, kw, preferred_element_type=f32) * (hd ** -0.5)
@@ -279,6 +279,35 @@
             out[:, lanes(g)] = total.astype(bf16)
             store(out.at[:, lanes(g)], (dk_hbm, dv_hbm)[i].at[:, lanes(g)])
 
+    parts = (pl.ds(0, groups - 1), pl.ds(groups - 1, 1))
+    bias_out = []
+
+    def bias_copy(phase, buf, slot, step, send_sem, recv_sem, device):
+        return pltpu.make_async_remote_copy(
+            src_ref=buf.at[slot, parts[phase]], dst_ref=buf.at[slot, parts[phase]],
+            send_sem=send_sem.at[phase, step], recv_sem=recv_sem.at[phase, step],
+            device_id=device, device_id_type=MESH)
+
+    def bias_send(phase, buf, mine, count, send_sem, recv_sem, device):
+        for step in range(1, count):
+            copy = bias_copy(phase, buf, mine, step, send_sem, recv_sem, device(lax.rem(mine + step, count)))
+            copy.start()
+            bias_out.append(copy)
+
+    def bias_wait(phase, buf, mine, count, send_sem, recv_sem, device):
+        for step in range(1, count):
+            source = lax.rem(mine + count - step, count)
+            bias_copy(phase, buf, source, step, send_sem, recv_sem, device(source)).wait_recv()
+
+    def bias_sum(phase):
+        total = bias_cols[0, parts[phase]]
+        for at in range(1, n_col):
+            total = total + bias_cols[at, parts[phase]]
+        bias_rows[r, parts[phase]] = total
+
+    by_col = (bias_cols, c, n_col, bc_s, bc_r, lambda at: (r, at))
+    by_row = (bias_rows, r, n_row, br_s, br_r, lambda at: (at, c))
+
     for g in range(groups):
         for d in range(2):
             for i in range(2):
@@ -295,53 +324,33 @@
             row_stage(g + 1)
         col_wait(g)
         compute(g)
+        if g >= groups - 2:
+            bias_send(g - groups + 2, *by_col)
         if g >= 1:
             col_return(g - 1)
         if g >= 2:
             finish(g - 2)
 
     store(dq_ref, dq_hbm)
-
-    def bias_copies(buf, mine, count, send_sem, recv_sem, device):
-        return [pltpu.make_async_remote_copy(
-            src_ref=buf.at[mine], dst_ref=buf.at[mine],
-            send_sem=send_sem.at[step], recv_sem=recv_sem.at[step],
-            device_id=device(lax.rem(mine + step, count)), device_id_type=MESH)
-            for step in range(1, count)]
-
-    def bias_waits(buf, mine, count, send_sem, recv_sem, device):
-        for step in range(1, count):
-            source = lax.rem(mine + count - step, count)
-            pltpu.make_async_remote_copy(
-                src_ref=buf.at[source], dst_ref=buf.at[source],
-                send_sem=send_sem.at[step], recv_sem=recv_sem.at[step],
-                device_id=device(source), device_id_type=MESH).wait_recv()
-
-    by_col = (bias_cols, c, n_col, bc_s, bc_r, lambda at: (r, at))
-    by_row = (bias_rows, r, n_row, br_s, br_r, lambda at: (at, c))
-    col_copies = bias_copies(*by_col)
-    for copy in col_copies:
-        copy.start()
+    bias_wait(0, *by_col)
+    bias_sum(0)
+    bias_send(0, *by_row)
     col_return(groups - 1)
-    if groups >= 2:
-        finish(groups - 2)
-    bias_waits(*by_col)
-    total = bias_cols[0]
-    for at in range(1, n_col):
-        total = total + bias_cols[at]
-    bias_rows[r] = total
-    row_copies = bias_copies(*by_row)
-    for copy in row_copies:
-        copy.start()
+    finish(groups - 2)
+    bias_wait(1, *by_col)
+    bias_sum(1)
+    bias_send(1, *by_row)
+    bias_wait(0, *by_row)
     finish(groups - 1)
-    bias_waits(*by_row)
-    total = bias_rows[0]
-    for at in range(1, n_row):
-        total = total + bias_rows[at]
-    for a in range(win):
-        db_ref[a] = total[:, a * pc:a * pc + win]
+    bias_wait(1, *by_row)
+    for g in range(groups):
+        total = bias_rows[0, g]
+        for at in range(1, n_row):
+            total = total + bias_rows[at, g]
+        for a in range(win):
+            db_ref[a, pl.ds(g * per, per), :] = total[:, a * pc:a * pc + win]
     store(db_ref, db_hbm)
-    for copy in col_copies + row_copies:
+    for copy in bias_out:
         copy.wait_send()
     for copy in stores:
         copy.wait()
@@ -408,14 +417,14 @@
             pltpu.VMEM((per * nq, span), bf16),
             pltpu.VMEM((per * nq, span), bf16),
             pltpu.VMEM((per, tc, span), f32),
-            pltpu.VMEM((n_col, heads, span), f32),
-            pltpu.VMEM((n_row, heads, span), f32),
+            pltpu.VMEM((n_col, groups, per, span), f32),
+            pltpu.VMEM((n_row, groups, per, span), f32),
             dma((2, groups, 2)), dma((2, groups, 2)),
             dma((2, groups, 3)), dma((2, groups, 3)),
             dma((2, groups)), dma((2, groups)),
             dma((2, groups)), dma((2, groups)),
-            dma((n_col,)), dma((n_col,)),
-            dma((n_row,)), dma((n_row,)),
+            dma((2, n_col)), dma((2, n_col)),
+            dma((2, n_row)), dma((2, n_row)),
         ],
         compiler_params=pltpu.CompilerParams(
             collective_id=0, has_side_effects=True),

time: 38.4 us -> 37.5 us (0.977)
  Pallas kernels: 37.6 us -> 36.7 us
    pallas_call x1, Pallas kernels: 35.9 us -> 34.9 us  [shards(): pl.pallas_call(functools.partial(kernel, cfg), out_shape=results, in_spec...]
where the time goes in v3:
time: 37.5 us; the launch traced here: 37.3 us
  Pallas kernels  36.7 us (98%)
  between operations  0.64 us (2%)
    pallas_call x1, Pallas kernels, shards(): pl.pallas_call(functools.partial(kernel, cfg), out_shape=results, in_spec...  34.9 us
    pallas_call x1, Pallas kernels, shards(): pl.pallas_call(writer, out_shape=results, in_specs=[hbm] * 4, out_specs=(...  1.78 us

profile of v3, /device:TPU:0, one launch (start us, length us, event | category | flops | bytes accessed | tf_op | source)
XLA Modules:
  0.0 37.3 jit_solution(8737827714667092363)
XLA Ops:
  0.6 34.9 %shard_map.93 = (bf16[128,512]{1,0:T(8,128)(2,1)}, bf16[128,512]{1,0:T(8,128)(2,1)}, bf16[128,512]{1,0:T(8,128)(2,1)}, f32[17,8,17]{2,1,0:T(8,128)}) custom-call(bf16[128,512]{1,0:T(8,128)(2,1)} %bitcast.9, bf16[128,512]{1,0:T(8,128)(2,1)} %bitcast.10, bf16[128,512]{1,0:T(8,128)(2,1)} %bitcast.11, bf16[128,512]{1,0:T(8,128)(2,1)} %bitcast.12, ...), custom_call_target="tpu_custom_call" | custom-call | tf_op jit(solution)/shard_map/pallas_call | solution.py:395
  35.5 1.8 %shard_map.94 = (bf16[128,512]{1,0:T(8,128)(2,1)}, bf16[128,512]{1,0:T(8,128)(2,1)}, bf16[128,512]{1,0:T(8,128)(2,1)}, f32[17,8,17]{2,1,0:T(8,128)}) custom-call(bf16[128,512]{1,0:T(8,128)(2,1)} %get-tuple-element.12.refs_0_, bf16[128,512]{1,0:T(8,128)(2,1)} %get-tuple-element.13.refs_1_, bf16[128,512]{1,0:T(8,128)(2,1)} %get-tuple-element.14.refs_2_, ...), custom_call_target="tpu_custom_call" | custom-call | tf_op jit(solution)/shard_map/pallas_call | solution.py:435
